TPU v7x, 32 devices: a whole 2x2x4 slice. The times are simulated.
32 devices in a mesh: groups: 2 (over y), tm: 4 (over z), dp: 2 (over x), width: 2 (over core).
Axes of the slice: x: 2, y: 2, z: 4, core: 2. Of those that a mesh axis runs over, the one named last changes fastest.
Arguments:
- clips: bfloat16 [4, 16, 8, 64, 128], P(('groups', 'dp'), 'tm', 'width'), parts along dimension 0, may hold values from -16.5 to 16.5
- gain: float32 [128], replicated, may hold values from 0.5 to 1.5
- bias: float32 [128], replicated, may hold values from -3 to 3
- weight: bfloat16 [3456, 256], replicated, may hold values from -0.109375 to 0.109375
- cotangent: bfloat16 [4, 16, 8, 64, 256], P(('groups', 'dp'), 'tm', 'width'), parts along dimension 0, may hold values from -6 to 6
Outputs:
- output: bfloat16 [4, 16, 8, 64, 256], P(('groups', 'dp'), 'tm', 'width'), parts along dimension 0
- grad_weight: float32 [6912, 256], P(('groups', 'tm', 'dp'), 'width'), parts along dimension 0
- grad_gain: float32 [256], P('groups'), parts along dimension 0
- grad_bias: float32 [256], P('groups'), parts along dimension 0
There are 2 independent parts, one for each index of `groups`. A program takes and returns all parts, laid end to end along the dimension named above; an argument that names none is the same for every part. Nothing has to cross between parts.
All inputs are finite; a program needn't handle non-finite values.
Results may differ from a plain program's by a relative error of at most 0.0049.
Values may be sent and summed in bfloat16 or wider, within the bound.
No kernel may reach another device: no remote copies, remote signals or barrier semaphores. Data moves between devices by JAX's collectives and lax.ppermute only.
A program may use at most 64 MiB of HBM per device.

v0:
```python
import jax
import jax.numpy as jnp
from jax import lax
from jax.sharding import PartitionSpec as P

GROUPS = 32


def prefix(value, axis, join, neutral):
    count, mine = (lax.axis_size(axis), lax.axis_index(axis))
    pieces = jax.tree.map(lambda part: lax.all_gather(part, axis), value)
    total = jax.tree.map(
        lambda part, zero: jnp.full_like(part, 0) + jnp.asarray(zero, part.dtype), value, neutral
    )

    def lap(position, total):
        longer = join(total, jax.tree.map(lambda part: part[position], pieces))
        return jax.tree.map(lambda new, old: jnp.where(position < mine, new, old), longer, total)

    return lax.fori_loop(0, count - 1, lap, total)


def with_halo(value, sides, width):
    for axis, dim in sides:
        devices, length = (lax.axis_size(axis), value.shape[dim])
        up = [(i, (i + 1) % devices) for i in range(devices - 1)]
        down = [(j, i) for i, j in up]
        last = lax.slice_in_dim(value, length - width, length, axis=dim)
        first = lax.slice_in_dim(value, 0, width, axis=dim)
        before = lax.ppermute(last, axis, up)
        after = lax.ppermute(first, axis, down)
        value = jnp.concatenate([before, value, after], axis=dim)
    return value


def from_behind(value, axis, steps):
    count = lax.axis_size(axis)
    first, last = (max(0, -steps), min(count, count - steps))
    return lax.ppermute(value, axis, [(source, source + steps) for source in range(first, last)])


def add_pair(earlier, later):
    return (earlier[0] + later[0], earlier[1] + later[1])


def body(clips, gain, bias, weight, cotangent):
    frames_in = clips[0]
    frame_count, row_count, col_count, chan_in = frames_in.shape
    chan_out = weight.shape[1]
    per_group = chan_in // GROUPS
    values = frames_in.astype(jnp.float32)
    grouped = values.reshape(frame_count, row_count, col_count, GROUPS, per_group)
    local_first = jnp.sum(grouped, axis=(1, 2, 4))
    local_square = jnp.sum(grouped * grouped, axis=(1, 2, 4))
    total_first, total_square = lax.psum((local_first, local_square), "width")
    zero_row = jnp.zeros((GROUPS,), jnp.float32)
    before_first, before_square = prefix(
        (jnp.sum(total_first, axis=0), jnp.sum(total_square, axis=0)),
        "tm",
        add_pair,
        (zero_row, zero_row),
    )
    first_sum = before_first + jnp.cumsum(total_first, axis=0)
    square_sum = before_square + jnp.cumsum(total_square, axis=0)
    frame_start = (lax.axis_index("tm") * frame_count).astype(jnp.float32)
    count = (frame_start + jnp.arange(frame_count, dtype=jnp.float32) + 1.0) * float(
        row_count * lax.axis_size("width") * col_count * per_group
    )
    mean = first_sum / count[:, None]
    variance = square_sum / count[:, None] - mean * mean
    inverse = lax.rsqrt(variance + 1e-05)
    normed = ((grouped - mean[:, None, None, :, None]) * inverse[:, None, None, :, None]).reshape(
        frame_count, row_count, col_count, chan_in
    )
    act = normed * gain + bias
    sigma = jax.nn.sigmoid(act)
    hidden = (act * sigma).astype(jnp.bfloat16)
    hidden_rows = with_halo(hidden, (("width", 1),), 1)
    earlier = from_behind(hidden_rows[frame_count - 2 :], "tm", 1)
    padded = jnp.pad(
        jnp.concatenate([earlier, hidden_rows], axis=0), ((0, 0), (0, 0), (1, 1), (0, 0))
    )
    pieces = []
    for lag_t in range(3):
        for row_off in range(3):
            for col_off in range(3):
                pieces.append(
                    padded[
                        lag_t : lag_t + frame_count,
                        row_off : row_off + row_count,
                        col_off : col_off + col_count,
                    ].reshape(-1, chan_in)
                )
    patches = jnp.concatenate(pieces, axis=1)
    output = jnp.dot(patches, weight, preferred_element_type=jnp.float32).astype(jnp.bfloat16)
    output = output.reshape(1, frame_count, row_count, col_count, chan_out)
    cot_local = cotangent[0]
    cot_rows = with_halo(cot_local, (("width", 1),), 1)
    later = from_behind(cot_rows[:2], "tm", -1)
    cot_padded = jnp.pad(
        jnp.concatenate([cot_rows, later], axis=0), ((0, 0), (0, 0), (1, 1), (0, 0))
    )
    kernel_taps = weight.reshape(27, chan_in, chan_out)
    grad_hidden = jnp.zeros((frame_count * row_count * col_count, chan_in), jnp.float32)
    for lag_t in range(3):
        for row_off in range(3):
            for col_off in range(3):
                tap_index = (lag_t * 3 + row_off) * 3 + col_off
                window = cot_padded[
                    2 - lag_t : 2 - lag_t + frame_count,
                    2 - row_off : 2 - row_off + row_count,
                    2 - col_off : 2 - col_off + col_count,
                ].reshape(-1, chan_out)
                grad_hidden = grad_hidden + lax.dot_general(
                    window,
                    kernel_taps[tap_index],
                    (((1,), (1,)), ((), ())),
                    preferred_element_type=jnp.float32,
                )
    grad_hidden = grad_hidden.reshape(frame_count, row_count, col_count, chan_in)
    grad_act = grad_hidden * sigma * (1.0 + act * (1.0 - sigma))
    grad_gain, grad_bias = lax.psum(
        (jnp.sum(grad_act * normed, axis=(0, 1, 2)), jnp.sum(grad_act, axis=(0, 1, 2))),
        ("tm", "dp", "width"),
    )
    cot_flat = cot_local.reshape(-1, chan_out)
    partial_rows = lax.psum_scatter(
        lax.dot_general(
            patches, cot_flat, (((0,), (0,)), ((), ())), preferred_element_type=jnp.float32
        ),
        ("tm", "dp"),
        scatter_dimension=0,
        tiled=True,
    )
    grad_weight = lax.psum_scatter(partial_rows, "width", scatter_dimension=1, tiled=True)
    return (output, grad_weight, grad_gain, grad_bias)


def solution(mesh):
    return jax.shard_map(
        body,
        mesh=mesh,
        in_specs=(
            P(("groups", "dp"), "tm", "width", None, None),
            P(),
            P(),
            P(),
            P(("groups", "dp"), "tm", "width", None, None),
        ),
        out_specs=(
            P(("groups", "dp"), "tm", "width", None, None),
            P(("groups", "tm", "dp"), "width"),
            P("groups"),
            P("groups"),
        ),
        check_vma=False,
    )
```

profile of v0, /device:TPU:0, one launch (start us, length us, event | category | flops | bytes accessed | tf_op | source)
XLA Modules:
  0.0 179.6 jit_solution(5625925412675377033)
XLA Ops:
  7.2 1.1 multiply_reduce_fusion.1
  8.3 0.1 reduce_sum.69
  8.4 0.1 reduce_sum.73
  8.6 0.1 reduce_sum.70
  8.7 0.1 reduce_sum.74
  8.8 2.6 %all-reduce.6 = (f32[4,32]{1,0:T(4,128)S(1)}, f32[4,32]{1,0:T(4,128)S(1)}) all-reduce(f32[4,32]{1,0:T(4,128)S(1)} %reduce_sum.70, f32[4,32]{1,0:T(4,128)S(1)} %reduce_sum.74), channel_id=1, replica_groups=mesh['groups'=2,'tm'=4,'dp'=2,'width'=2] {'width'}, use_global_device_ids=true, to_apply=%region_2.0 | all-reduce | flops 256 | bytes 2048 | tf_op jit(solution)/shard_map/psum | solution.py:55
  11.4 1.2 dynamic-slice
  13.3 0.2 dynamic-update-slice
  13.6 0.2 dynamic-update-slice.1
  13.8 13.3 %all-reduce.5 = (f32[128]{0:T(128)S(1)}, f32[128]{0:T(128)S(1)}) all-reduce(f32[128]{0:T(128)S(1)} %dynamic-update-slice, f32[128]{0:T(128)S(1)} %dynamic-update-slice.1), channel_id=2, replica_groups=mesh['groups'=2,'tm'=4,'dp'=2,'width'=2] {'tm'}, use_global_device_ids=true, to_apply=%add.2 | all-reduce | flops 256 | bytes 2048
  27.0 0.1 reshape.401
  27.2 0.1 while.16
  27.5 0.1 mul.86
  27.7 0.1 sub.33
  27.8 1.2 multiply_convert_fusion.1
  29.0 1.3 collective-permute-start.1
  30.3 3.0 %collective-permute-start = (bf16[4,1,64,128]{3,2,1,0:T(8,128)(2,1)S(1)}, bf16[4,1,64,128]{3,2,1,0:T(8,128)(2,1)S(1)}, u32[]{:S(2)}, u32[]{:S(2)}) collective-permute-start(bf16[4,1,64,128]{3,2,1,0:T(8,128)(2,1)S(1)} %get-tuple-element.217), channel_id=1, source_target_pairs={{0,1},{2,3},{4,5},{6,7},{8,9},{10,11},{12,13},{14,15},{16,17},{18,... | collective-permute-start | bytes 196616 | tf_op jit(solution)/shard_map/ppermute | solution.py:30
  33.4 1.0 fusion.41
  34.4 1.3 collective-permute-start.4
  35.7 3.0 %collective-permute-start.3 = (bf16[4,1,64,256]{3,2,1,0:T(8,128)(2,1)S(1)}, bf16[4,1,64,256]{3,2,1,0:T(8,128)(2,1)S(1)}, u32[]{:S(2)}, u32[]{:S(2)}) collective-permute-start(bf16[4,1,64,256]{3,2,1,0:T(8,128)(2,1)S(1)} %get-tuple-element.213), channel_id=1, source_target_pairs={{0,1},{2,3},{4,5},{6,7},{8,9},{10,11},{12,13},{14,15},{16,17},{18,... | collective-permute-start | bytes 393224 | tf_op jit(solution)/shard_map/ppermute | solution.py:30
  38.8 1.3 collective-permute-start.2
  40.2 1.3 collective-permute-start.5
  41.6 2.4 %collective-permute-done.2 = bf16[2,6,64,128]{3,2,1,0:T(8,128)(2,1)S(1)} collective-permute-done((bf16[2,6,64,128]{3,2,1,0:T(8,128)(2,1)S(1)}, bf16[2,6,64,128]{3,2,1,0:T(8,128)(2,1)S(1)}, u32[]{:S(2)}, u32[]{:S(2)}) %collective-permute-start.2) | collective-permute-done | bytes 196640 | tf_op jit(solution)/shard_map/ppermute | solution.py:39
  44.1 0.2 fusion.40
  44.3 0.7 pad_slice_fusion
  45.1 0.7 pad_slice_fusion.1
  47.4 1.0 fusion.7
  48.7 2.9 %copy-done.5 = bf16[1024,3456]{1,0:T(8,128)(2,1)} copy-done((bf16[1024,3456]{1,0:T(8,128)(2,1)}, bf16[1024,3456]{1,0:T(8,128)(2,1)S(1)}, u32[]{:S(2)}) %copy-start.5) | copy-done | bytes 7077912
  51.6 3.9 %fusion.43 = f32[3456,256]{1,0:T(8,128)} fusion(bf16[1024,3456]{1,0:T(8,128)(2,1)S(1)} %constant_dynamic-update-slice_fusion, bf16[1024,256]{1,0:T(8,128)(2,1)S(1)} %bitcast.120), kind=kOutput, calls=%fused_computation.158 | convolution fusion | flops 1811939328 | bytes 11141120 | tf_op jit(solution)/shard_map/dot_general | solution.py:128
  55.6 0.2 reduce-scatter.5.cloned.1.call-start
  55.8 6.3 %convolution_convert_fusion = bf16[1024,256]{1,0:T(8,128)(2,1)} fusion(bf16[1024,3456]{1,0:T(8,128)(2,1)} %copy-done.5, bf16[3456,256]{1,0:T(8,128)(2,1)} %param.10), kind=kOutput, calls=%fused_computation.4 | convolution fusion | flops 1812201472 | bytes 9371648 | tf_op jit(solution)/shard_map/dot_general | solution.py:95
  62.1 0.2 pad_maximum_fusion
  62.3 2.6 %pad_slice_fusion.20 = (bf16[4,4,64,256]{3,2,1,0:T(8,128)(2,1)S(1)}, bf16[4,4,64,256]{3,2,1,0:T(8,128)(2,1)S(1)}, bf16[4,4,64,256]{3,2,1,0:T(8,128)(2,1)S(1)}, b...) fusion(bf16[6,6,64,256]{3,2,1,0:T(8,128)(2,1)S(1)} %pad_maximum, ...), kind=kLoop, calls=%fused_computation.137 | loop fusion | bytes 8519680 | tf_op jit(solution)/shard_map/slice | solution.py:109
  65.0 0.3 fusion.15
  65.2 0.3 fusion.39
  65.5 0.3 fusion.36
  65.8 0.3 convolution_add_fusion.23
  66.1 2.1 %pad_slice_fusion.19 = (bf16[4,4,64,256]{3,2,1,0:T(8,128)(2,1)}, bf16[4,4,64,256]{3,2,1,0:T(8,128)(2,1)S(1)}, bf16[4,4,64,256]{3,2,1,0:T(8,128)(2,1)S(1)}, bf16[...) fusion(bf16[6,6,64,256]{3,2,1,0:T(8,128)(2,1)S(1)} %pad_maximum, ...), kind=kLoop, calls=%fused_computation.136 | loop fusion | bytes 6946816 | tf_op jit(solution)/shard_map/slice | solution.py:109
  68.2 0.3 convolution_add_fusion.22
  68.5 0.3 convolution_add_fusion.21
  68.8 0.3 convolution_add_fusion.20
  69.1 0.3 convolution_add_fusion.19
  69.4 0.3 convolution_add_fusion.18
  69.7 0.3 convolution_add_fusion.17
  70.0 0.3 convolution_add_fusion.16
  70.3 0.3 convolution_add_fusion.15
  70.6 0.3 convolution_add_fusion.14
  71.0 0.3 convolution_add_fusion.13
  71.3 0.3 convolution_add_fusion.12
  71.6 0.3 convolution_add_fusion.11
  71.9 0.3 convolution_add_fusion.10
  72.2 0.3 convolution_add_fusion.9
  72.5 0.3 convolution_add_fusion.8
  72.8 0.3 convolution_add_fusion.7
  73.1 0.3 convolution_add_fusion.6
  73.4 0.3 fusion.3
  73.7 0.3 convolution_add_fusion.4
  74.0 60.9 %reduce-scatter.3.cloned.1.call-done = f32[432,256]{1,0:T(8,128)} async-done(((f32[3456,256]{1,0:T(8,128)}), f32[432,256]{1,0:T(8,128)}) %reduce-scatter.3.cloned.1.call-update) | async-done | bytes 442384 | tf_op jit(solution)/shard_map/reduce_scatter | solution.py:127
  134.9 1.2 fusion.8
  136.1 1.1 convolution_add_fusion.3
  137.2 1.1 convolution_add_fusion.2
  138.4 1.1 convolution_add_fusion.1
  139.5 1.3 fusion.38
  140.8 31.9 %all-reduce.4 = (f32[128]{0:T(128)}, f32[128]{0:T(128)}) all-reduce(f32[128]{0:T(128)S(1)} %get-tuple-element.138, f32[128]{0:T(128)S(1)} %get-tuple-element.137), channel_id=1, replica_groups=mesh['groups'=2,'tm'=4,'dp'=2,'width'=2] {'tm','dp','width'}, use_global_device_ids=true, to_apply=%region_15.16 | all-reduce | flops 256 | bytes 2048 | tf_op jit(solution)/shard_map/psum | solution.py:122
  (72 shorter events, 2.6 us)
Async XLA Ops:
  7.2 33.0 %copy-start = (bf16[1,4,4,64,256]{4,3,2,1,0:T(8,128)(2,1)S(1)}, bf16[1,4,4,64,256]{4,3,2,1,0:T(8,128)(2,1)}, u32[]{:S(2)}) copy-start(bf16[1,4,4,64,256]{4,3,2,1,0:T(8,128)(2,1)} %param.11) | copy-start | bytes 1572868
  7.2 127.7 %reduce-scatter.3.cloned.1.call-start = ((), (), s32[]{:S(2)}) async-start(), calls=%async_computation.2 | async-start | bytes 3981312 | tf_op jit(solution)/shard_map/reduce_scatter | solution.py:127
  29.0 9.7 %collective-permute-start.1 = (bf16[4,1,64,128]{3,2,1,0:T(8,128)(2,1)S(1)}, bf16[4,1,64,128]{3,2,1,0:T(8,128)(2,1)S(1)}, u32[]{:S(2)}, u32[]{:S(2)}) collective-permute-start(bf16[4,1,64,128]{3,2,1,0:T(8,128)(2,1)S(1)} %get-tuple-element.218), channel_id=1, source_target_pairs={{1,0},{3,2},{5,4},{7,6},{9,8},{11,10},{13,12},{15,14},{17,16},{19,... | collective-permute-start | bytes 196616 | tf_op jit(solution)/shard_map/ppermute | solution.py:31
  30.3 8.4 %collective-permute-start = (bf16[4,1,64,128]{3,2,1,0:T(8,128)(2,1)S(1)}, bf16[4,1,64,128]{3,2,1,0:T(8,128)(2,1)S(1)}, u32[]{:S(2)}, u32[]{:S(2)}) collective-permute-start(bf16[4,1,64,128]{3,2,1,0:T(8,128)(2,1)S(1)} %get-tuple-element.217), channel_id=1, source_target_pairs={{0,1},{2,3},{4,5},{6,7},{8,9},{10,11},{12,13},{14,15},{16,17},{18,... | collective-permute-start | bytes 196616 | tf_op jit(solution)/shard_map/ppermute | solution.py:30
  34.4 5.8 %collective-permute-start.4 = (bf16[4,1,64,256]{3,2,1,0:T(8,128)(2,1)S(1)}, bf16[4,1,64,256]{3,2,1,0:T(8,128)(2,1)S(1)}, u32[]{:S(2)}, u32[]{:S(2)}) collective-permute-start(bf16[4,1,64,256]{3,2,1,0:T(8,128)(2,1)S(1)} %get-tuple-element.214), channel_id=1, source_target_pairs={{1,0},{3,2},{5,4},{7,6},{9,8},{11,10},{13,12},{15,14},{17,16},{19,... | collective-permute-start | bytes 393224 | tf_op jit(solution)/shard_map/ppermute | solution.py:31
  35.7 4.5 %collective-permute-start.3 = (bf16[4,1,64,256]{3,2,1,0:T(8,128)(2,1)S(1)}, bf16[4,1,64,256]{3,2,1,0:T(8,128)(2,1)S(1)}, u32[]{:S(2)}, u32[]{:S(2)}) collective-permute-start(bf16[4,1,64,256]{3,2,1,0:T(8,128)(2,1)S(1)} %get-tuple-element.213), channel_id=1, source_target_pairs={{0,1},{2,3},{4,5},{6,7},{8,9},{10,11},{12,13},{14,15},{16,17},{18,... | collective-permute-start | bytes 393224 | tf_op jit(solution)/shard_map/ppermute | solution.py:30
  38.8 5.3 %collective-permute-start.2 = (bf16[2,6,64,128]{3,2,1,0:T(8,128)(2,1)S(1)}, bf16[2,6,64,128]{3,2,1,0:T(8,128)(2,1)S(1)}, u32[]{:S(2)}, u32[]{:S(2)}) collective-permute-start(bf16[2,6,64,128]{3,2,1,0:T(8,128)(2,1)S(1)} %pad_maximum_fusion.7), channel_id=1, source_target_pairs={{0,4},{4,8},{8,12},{1,5},{5,9},{9,13},{2,6},{6,10},{10,14},{3,7},{... | collective-permute-start | bytes 589832 | tf_op jit(solution)/shard_map/ppermute | solution.py:39
  40.2 21.9 %collective-permute-start.5 = (bf16[2,6,64,256]{3,2,1,0:T(8,128)(2,1)S(1)}, bf16[2,6,64,256]{3,2,1,0:T(8,128)(2,1)S(1)}, u32[]{:S(2)}, u32[]{:S(2)}) collective-permute-start(bf16[2,6,64,256]{3,2,1,0:T(8,128)(2,1)S(1)} %pad_maximum_fusion.3), channel_id=1, source_target_pairs={{4,0},{8,4},{12,8},{5,1},{9,5},{13,9},{6,2},{10,6},{14,10},{7,3},{... | collective-permute-start | bytes 1179656 | tf_op jit(solution)/shard_map/ppermute | solution.py:39
  46.4 1.0 copy-start.1
  46.4 1.0 copy-start.6
  46.4 1.0 copy-start.7
  48.7 2.9 %copy-start.5 = (bf16[1024,3456]{1,0:T(8,128)(2,1)}, bf16[1024,3456]{1,0:T(8,128)(2,1)S(1)}, u32[]{:S(2)}) copy-start(bf16[1024,3456]{1,0:T(8,128)(2,1)S(1)} %constant_dynamic-update-slice_fusion) | copy-start | bytes 21233668
  55.6 117.2 %reduce-scatter.5.cloned.1.call-start = ((), (), s32[]{:S(2)}) async-start(), calls=%async_computation.3 | async-start | bytes 663552 | tf_op jit(solution)/shard_map/reduce_scatter | solution.py:135
  62.3 2.7 %copy-start.4 = (bf16[3456,256]{1,0:T(8,128)(2,1)S(1)}, bf16[3456,256]{1,0:T(8,128)(2,1)}, u32[]{:S(2)}) copy-start(bf16[3456,256]{1,0:T(8,128)(2,1)} %param.10) | copy-start | bytes 5308420
  74.0 65.5 %copy-start.2 = (f32[1024,128]{1,0:T(8,128)S(1)}, f32[1024,128]{1,0:T(8,128)}, u32[]{:S(2)}) copy-start(f32[1024,128]{1,0:T(8,128)} %get-tuple-element.220) | copy-start | bytes 1572868
  134.9 3.5 %copy-start.3 = (bf16[4,4,64,256]{3,2,1,0:T(8,128)(2,1)S(1)}, bf16[4,4,64,256]{3,2,1,0:T(8,128)(2,1)}, u32[]{:S(2)}) copy-start(bf16[4,4,64,256]{3,2,1,0:T(8,128)(2,1)} %get-tuple-element.163) | copy-start | bytes 1572868
Sparse Core Ops, SparseCore 0:
  55.7 79.1 reduce-scatter.2
  137.7 7.3 reduce-scatter.4
where the time goes:
time: 180 us
  waiting for transfers between devices  63.3 us (35%)
  blocking collectives  47.8 us (27%)
  matrix products  22.7 us (13%)
  between operations  15.4 us (9%)
  local copies, waits for them, and re-layouts  14.7 us (8%)
  starting transfers between devices  11.5 us (6%)
  other arithmetic  4.15 us (2%)
    reduce_scatter x1, waiting for transfers between devices, body(): lax.psum_scatter(lax.dot_general(patches, cot_flat, (((0,), (0,)), ((), (...  60.9 us
    psum x1, blocking collectives, body(): lax.psum((jnp.sum(grad_act * normed, axis=(0, 1, 2)), jnp.sum(grad_act, a...  31.9 us
    unnamed x1, blocking collectives  13.3 us
    dot_general x27, matrix products, body(): lax.dot_general(window, kernel_taps[tap_index], (((1,), (1,)), ((), ())),...  12.5 us
    dot_general x1, matrix products, body(): jnp.dot(patches, weight, preferred_element_type=jnp.float32)  6.34 us
    unnamed x46, local copies, waits for them, and re-layouts  6.22 us
    ppermute x2, starting transfers between devices, with_halo(): before = lax.ppermute(last, axis, up)  6.07 us
    slice x3, local copies, waits for them, and re-layouts, body(): cot_padded[2 - lag_t:2 - lag_t + frame_count, 2 - row_off:2 - row_off + r...  5.01 us
  transfers between devices with their start and end apart: 8, of which 2 were waited for; matrix products, arithmetic and copies ran while one was open for 19% of the time, Pallas kernels for 0%

commit v1 on v0

--- a/solution.py
+++ b/solution.py
@@ -1,9 +1,19 @@
+import functools
 import jax
 import jax.numpy as jnp
 from jax import lax
 from jax.sharding import PartitionSpec as P
 
 GROUPS = 32
+
+
+def produce_strings(load, axis_name, mesh_dim):
+    for m in (axis_name, mesh_dim):
+        load = lax.psum(load, m)
+    return load
+
+
+lift_shapes = functools.partial(produce_strings, axis_name=("dp", "width"), mesh_dim="tm")
 
 
 def prefix(value, axis, join, neutral):
@@ -119,9 +129,8 @@
                 )
     grad_hidden = grad_hidden.reshape(frame_count, row_count, col_count, chan_in)
     grad_act = grad_hidden * sigma * (1.0 + act * (1.0 - sigma))
-    grad_gain, grad_bias = lax.psum(
-        (jnp.sum(grad_act * normed, axis=(0, 1, 2)), jnp.sum(grad_act, axis=(0, 1, 2))),
-        ("tm", "dp", "width"),
+    grad_gain, grad_bias = lift_shapes(
+        (jnp.sum(grad_act * normed, axis=(0, 1, 2)), jnp.sum(grad_act, axis=(0, 1, 2)))
     )
     cot_flat = cot_local.reshape(-1, chan_out)
     partial_rows = lax.psum_scatter(

time: 180 us -> 165 us (0.917)
  blocking collectives: 47.8 us -> 32.9 us
    psum x1 -> x2, blocking collectives: 31.9 us -> 17 us  [produce_strings(): load = lax.psum(load, m)]
  transfers between devices with their start and end apart: 8 -> 8, of which waited for: 2 -> 2; matrix products, arithmetic and copies ran while one was open for 19% -> 20% of each run, Pallas kernels for 0% -> 0%
where the time goes in v1:
time: 165 us
  waiting for transfers between devices  63.3 us (38%)
  blocking collectives  32.9 us (20%)
  matrix products  22.7 us (14%)
  between operations  15.4 us (9%)
  local copies, waits for them, and re-layouts  14.7 us (9%)
  starting transfers between devices  11.5 us (7%)
  other arithmetic  4.15 us (3%)
    reduce_scatter x1, waiting for transfers between devices, body(): lax.psum_scatter(lax.dot_general(patches, cot_flat, (((0,), (0,)), ((), (...  60.9 us
    psum x2, blocking collectives, produce_strings(): load = lax.psum(load, m)  17 us
    unnamed x1, blocking collectives  13.3 us
    dot_general x27, matrix products, body(): lax.dot_general(window, kernel_taps[tap_index], (((1,), (1,)), ((), ())),...  12.5 us
    dot_general x1, matrix products, body(): jnp.dot(patches, weight, preferred_element_type=jnp.float32)  6.34 us
    unnamed x46, local copies, waits for them, and re-layouts  6.22 us
    ppermute x2, starting transfers between devices, with_halo(): before = lax.ppermute(last, axis, up)  6.07 us
    slice x3, local copies, waits for them, and re-layouts, body(): cot_padded[2 - lag_t:2 - lag_t + frame_count, 2 - row_off:2 - row_off + r...  5.01 us
  transfers between devices with their start and end apart: 8, of which 2 were waited for; matrix products, arithmetic and copies ran while one was open for 20% of the time, Pallas kernels for 0%

profile of v1, /device:TPU:0, one launch (start us, length us, event | category | flops | bytes accessed | tf_op | source)
XLA Modules:
  0.0 164.7 jit_solution(473734962912098783)
XLA Ops:
  7.2 1.1 multiply_reduce_fusion.1
  8.3 0.1 reduce_sum.69
  8.4 0.1 reduce_sum.73
  8.6 0.1 reduce_sum.70
  8.7 0.1 reduce_sum.74
  8.8 2.6 %all-reduce.7 = (f32[4,32]{1,0:T(4,128)S(1)}, f32[4,32]{1,0:T(4,128)S(1)}) all-reduce(f32[4,32]{1,0:T(4,128)S(1)} %reduce_sum.70, f32[4,32]{1,0:T(4,128)S(1)} %reduce_sum.74), channel_id=1, replica_groups=mesh['groups'=2,'tm'=4,'dp'=2,'width'=2] {'width'}, use_global_device_ids=true, to_apply=%region_2.0 | all-reduce | flops 256 | bytes 2048 | tf_op jit(solution)/shard_map/psum | solution.py:65
  11.4 1.2 dynamic-slice
  13.3 0.2 dynamic-update-slice
  13.6 0.2 dynamic-update-slice.1
  13.8 13.3 %all-reduce.6 = (f32[128]{0:T(128)S(1)}, f32[128]{0:T(128)S(1)}) all-reduce(f32[128]{0:T(128)S(1)} %dynamic-update-slice, f32[128]{0:T(128)S(1)} %dynamic-update-slice.1), channel_id=2, replica_groups=mesh['groups'=2,'tm'=4,'dp'=2,'width'=2] {'tm'}, use_global_device_ids=true, to_apply=%add.2 | all-reduce | flops 256 | bytes 2048
  27.2 0.1 while.16
  27.5 0.1 mul.86
  27.7 0.1 sub.33
  27.8 1.2 multiply_convert_fusion.1
  29.0 1.3 collective-permute-start.1
  30.3 3.0 %collective-permute-start = (bf16[4,1,64,128]{3,2,1,0:T(8,128)(2,1)S(1)}, bf16[4,1,64,128]{3,2,1,0:T(8,128)(2,1)S(1)}, u32[]{:S(2)}, u32[]{:S(2)}) collective-permute-start(bf16[4,1,64,128]{3,2,1,0:T(8,128)(2,1)S(1)} %get-tuple-element.219), channel_id=1, source_target_pairs={{0,1},{2,3},{4,5},{6,7},{8,9},{10,11},{12,13},{14,15},{16,17},{18,... | collective-permute-start | bytes 196616 | tf_op jit(solution)/shard_map/ppermute | solution.py:40
  33.4 1.0 fusion.41
  34.4 1.3 collective-permute-start.4
  35.7 3.0 %collective-permute-start.3 = (bf16[4,1,64,256]{3,2,1,0:T(8,128)(2,1)S(1)}, bf16[4,1,64,256]{3,2,1,0:T(8,128)(2,1)S(1)}, u32[]{:S(2)}, u32[]{:S(2)}) collective-permute-start(bf16[4,1,64,256]{3,2,1,0:T(8,128)(2,1)S(1)} %get-tuple-element.215), channel_id=1, source_target_pairs={{0,1},{2,3},{4,5},{6,7},{8,9},{10,11},{12,13},{14,15},{16,17},{18,... | collective-permute-start | bytes 393224 | tf_op jit(solution)/shard_map/ppermute | solution.py:40
  38.8 1.3 collective-permute-start.2
  40.2 1.3 collective-permute-start.5
  41.6 2.4 %collective-permute-done.2 = bf16[2,6,64,128]{3,2,1,0:T(8,128)(2,1)S(1)} collective-permute-done((bf16[2,6,64,128]{3,2,1,0:T(8,128)(2,1)S(1)}, bf16[2,6,64,128]{3,2,1,0:T(8,128)(2,1)S(1)}, u32[]{:S(2)}, u32[]{:S(2)}) %collective-permute-start.2) | collective-permute-done | bytes 196640 | tf_op jit(solution)/shard_map/ppermute | solution.py:49
  44.1 0.2 fusion.40
  44.3 0.7 pad_slice_fusion
  45.1 0.7 pad_slice_fusion.1
  47.4 1.0 fusion.7
  48.7 2.9 %copy-done.5 = bf16[1024,3456]{1,0:T(8,128)(2,1)} copy-done((bf16[1024,3456]{1,0:T(8,128)(2,1)}, bf16[1024,3456]{1,0:T(8,128)(2,1)S(1)}, u32[]{:S(2)}) %copy-start.5) | copy-done | bytes 7077912
  51.6 3.9 %fusion.43 = f32[3456,256]{1,0:T(8,128)} fusion(bf16[1024,3456]{1,0:T(8,128)(2,1)S(1)} %constant_dynamic-update-slice_fusion, bf16[1024,256]{1,0:T(8,128)(2,1)S(1)} %bitcast.120), kind=kOutput, calls=%fused_computation.158 | convolution fusion | flops 1811939328 | bytes 11141120 | tf_op jit(solution)/shard_map/dot_general | solution.py:137
  55.6 0.2 reduce-scatter.5.cloned.1.call-start
  55.8 6.3 %convolution_convert_fusion = bf16[1024,256]{1,0:T(8,128)(2,1)} fusion(bf16[1024,3456]{1,0:T(8,128)(2,1)} %copy-done.5, bf16[3456,256]{1,0:T(8,128)(2,1)} %param.10), kind=kOutput, calls=%fused_computation.4 | convolution fusion | flops 1812201472 | bytes 9371648 | tf_op jit(solution)/shard_map/dot_general | solution.py:105
  62.1 0.2 pad_maximum_fusion
  62.3 2.6 %pad_slice_fusion.20 = (bf16[4,4,64,256]{3,2,1,0:T(8,128)(2,1)S(1)}, bf16[4,4,64,256]{3,2,1,0:T(8,128)(2,1)S(1)}, bf16[4,4,64,256]{3,2,1,0:T(8,128)(2,1)S(1)}, b...) fusion(bf16[6,6,64,256]{3,2,1,0:T(8,128)(2,1)S(1)} %pad_maximum, ...), kind=kLoop, calls=%fused_computation.137 | loop fusion | bytes 8519680 | tf_op jit(solution)/shard_map/slice | solution.py:119
  65.0 0.3 fusion.15
  65.2 0.3 fusion.39
  65.5 0.3 fusion.36
  65.8 0.3 convolution_add_fusion.23
  66.1 2.1 %pad_slice_fusion.19 = (bf16[4,4,64,256]{3,2,1,0:T(8,128)(2,1)}, bf16[4,4,64,256]{3,2,1,0:T(8,128)(2,1)S(1)}, bf16[4,4,64,256]{3,2,1,0:T(8,128)(2,1)S(1)}, bf16[...) fusion(bf16[6,6,64,256]{3,2,1,0:T(8,128)(2,1)S(1)} %pad_maximum, ...), kind=kLoop, calls=%fused_computation.136 | loop fusion | bytes 6946816 | tf_op jit(solution)/shard_map/slice | solution.py:119
  68.2 0.3 convolution_add_fusion.22
  68.5 0.3 convolution_add_fusion.21
  68.8 0.3 convolution_add_fusion.20
  69.1 0.3 convolution_add_fusion.19
  69.4 0.3 convolution_add_fusion.18
  69.7 0.3 convolution_add_fusion.17
  70.0 0.3 convolution_add_fusion.16
  70.3 0.3 convolution_add_fusion.15
  70.6 0.3 convolution_add_fusion.14
  71.0 0.3 convolution_add_fusion.13
  71.3 0.3 convolution_add_fusion.12
  71.6 0.3 convolution_add_fusion.11
  71.9 0.3 convolution_add_fusion.10
  72.2 0.3 convolution_add_fusion.9
  72.5 0.3 convolution_add_fusion.8
  72.8 0.3 convolution_add_fusion.7
  73.1 0.3 convolution_add_fusion.6
  73.4 0.3 fusion.3
  73.7 0.3 convolution_add_fusion.4
  74.0 60.9 %reduce-scatter.3.cloned.1.call-done = f32[432,256]{1,0:T(8,128)} async-done(((f32[3456,256]{1,0:T(8,128)}), f32[432,256]{1,0:T(8,128)}) %reduce-scatter.3.cloned.1.call-update) | async-done | bytes 442384 | tf_op jit(solution)/shard_map/reduce_scatter | solution.py:136
  134.9 1.2 fusion.8
  136.1 1.1 convolution_add_fusion.3
  137.2 1.1 convolution_add_fusion.2
  138.4 1.1 convolution_add_fusion.1
  139.5 1.3 fusion.38
  140.8 6.2 %all-reduce.4 = (f32[128]{0:T(128)S(1)}, f32[128]{0:T(128)S(1)}) all-reduce(f32[128]{0:T(128)S(1)} %get-tuple-element.138, f32[128]{0:T(128)S(1)} %get-tuple-element.137), channel_id=1, replica_groups=mesh['groups'=2,'tm'=4,'dp'=2,'width'=2] {'dp','width'}, use_global_device_ids=true, to_apply=%region_15.16 | all-reduce | flops 256 | bytes 2048 | tf_op jit(solution)/shard_map/psum | solution.py:12
  147.1 10.8 %all-reduce.5 = (f32[128]{0:T(128)}, f32[128]{0:T(128)}) all-reduce(f32[128]{0:T(128)S(1)} %get-tuple-element.153, f32[128]{0:T(128)S(1)} %get-tuple-element.154), channel_id=1, replica_groups=mesh['groups'=2,'tm'=4,'dp'=2,'width'=2] {'tm'}, use_global_device_ids=true, to_apply=%region_16.17 | all-reduce | flops 256 | bytes 2048 | tf_op jit(solution)/shard_map/psum | solution.py:12
  (73 shorter events, 2.6 us)
Async XLA Ops:
  7.2 33.0 %copy-start = (bf16[1,4,4,64,256]{4,3,2,1,0:T(8,128)(2,1)S(1)}, bf16[1,4,4,64,256]{4,3,2,1,0:T(8,128)(2,1)}, u32[]{:S(2)}) copy-start(bf16[1,4,4,64,256]{4,3,2,1,0:T(8,128)(2,1)} %param.11) | copy-start | bytes 1572868
  7.2 127.7 %reduce-scatter.3.cloned.1.call-start = ((), (), s32[]{:S(2)}) async-start(), calls=%async_computation.2 | async-start | bytes 3981312 | tf_op jit(solution)/shard_map/reduce_scatter | solution.py:136
  29.0 9.7 %collective-permute-start.1 = (bf16[4,1,64,128]{3,2,1,0:T(8,128)(2,1)S(1)}, bf16[4,1,64,128]{3,2,1,0:T(8,128)(2,1)S(1)}, u32[]{:S(2)}, u32[]{:S(2)}) collective-permute-start(bf16[4,1,64,128]{3,2,1,0:T(8,128)(2,1)S(1)} %get-tuple-element.220), channel_id=1, source_target_pairs={{1,0},{3,2},{5,4},{7,6},{9,8},{11,10},{13,12},{15,14},{17,16},{19,... | collective-permute-start | bytes 196616 | tf_op jit(solution)/shard_map/ppermute | solution.py:41
  30.3 8.4 %collective-permute-start = (bf16[4,1,64,128]{3,2,1,0:T(8,128)(2,1)S(1)}, bf16[4,1,64,128]{3,2,1,0:T(8,128)(2,1)S(1)}, u32[]{:S(2)}, u32[]{:S(2)}) collective-permute-start(bf16[4,1,64,128]{3,2,1,0:T(8,128)(2,1)S(1)} %get-tuple-element.219), channel_id=1, source_target_pairs={{0,1},{2,3},{4,5},{6,7},{8,9},{10,11},{12,13},{14,15},{16,17},{18,... | collective-permute-start | bytes 196616 | tf_op jit(solution)/shard_map/ppermute | solution.py:40
  34.4 5.8 %collective-permute-start.4 = (bf16[4,1,64,256]{3,2,1,0:T(8,128)(2,1)S(1)}, bf16[4,1,64,256]{3,2,1,0:T(8,128)(2,1)S(1)}, u32[]{:S(2)}, u32[]{:S(2)}) collective-permute-start(bf16[4,1,64,256]{3,2,1,0:T(8,128)(2,1)S(1)} %get-tuple-element.216), channel_id=1, source_target_pairs={{1,0},{3,2},{5,4},{7,6},{9,8},{11,10},{13,12},{15,14},{17,16},{19,... | collective-permute-start | bytes 393224 | tf_op jit(solution)/shard_map/ppermute | solution.py:41
  35.7 4.5 %collective-permute-start.3 = (bf16[4,1,64,256]{3,2,1,0:T(8,128)(2,1)S(1)}, bf16[4,1,64,256]{3,2,1,0:T(8,128)(2,1)S(1)}, u32[]{:S(2)}, u32[]{:S(2)}) collective-permute-start(bf16[4,1,64,256]{3,2,1,0:T(8,128)(2,1)S(1)} %get-tuple-element.215), channel_id=1, source_target_pairs={{0,1},{2,3},{4,5},{6,7},{8,9},{10,11},{12,13},{14,15},{16,17},{18,... | collective-permute-start | bytes 393224 | tf_op jit(solution)/shard_map/ppermute | solution.py:40
  38.8 5.3 %collective-permute-start.2 = (bf16[2,6,64,128]{3,2,1,0:T(8,128)(2,1)S(1)}, bf16[2,6,64,128]{3,2,1,0:T(8,128)(2,1)S(1)}, u32[]{:S(2)}, u32[]{:S(2)}) collective-permute-start(bf16[2,6,64,128]{3,2,1,0:T(8,128)(2,1)S(1)} %pad_maximum_fusion.7), channel_id=1, source_target_pairs={{0,4},{4,8},{8,12},{1,5},{5,9},{9,13},{2,6},{6,10},{10,14},{3,7},{... | collective-permute-start | bytes 589832 | tf_op jit(solution)/shard_map/ppermute | solution.py:49
  40.2 21.9 %collective-permute-start.5 = (bf16[2,6,64,256]{3,2,1,0:T(8,128)(2,1)S(1)}, bf16[2,6,64,256]{3,2,1,0:T(8,128)(2,1)S(1)}, u32[]{:S(2)}, u32[]{:S(2)}) collective-permute-start(bf16[2,6,64,256]{3,2,1,0:T(8,128)(2,1)S(1)} %pad_maximum_fusion.3), channel_id=1, source_target_pairs={{4,0},{8,4},{12,8},{5,1},{9,5},{13,9},{6,2},{10,6},{14,10},{7,3},{... | collective-permute-start | bytes 1179656 | tf_op jit(solution)/shard_map/ppermute | solution.py:49
  46.4 1.0 copy-start.1
  46.4 1.0 copy-start.6
  46.4 1.0 copy-start.7
  48.7 2.9 %copy-start.5 = (bf16[1024,3456]{1,0:T(8,128)(2,1)}, bf16[1024,3456]{1,0:T(8,128)(2,1)S(1)}, u32[]{:S(2)}) copy-start(bf16[1024,3456]{1,0:T(8,128)(2,1)S(1)} %constant_dynamic-update-slice_fusion) | copy-start | bytes 21233668
  55.6 102.3 %reduce-scatter.5.cloned.1.call-start = ((), (), s32[]{:S(2)}) async-start(), calls=%async_computation.3 | async-start | bytes 663552 | tf_op jit(solution)/shard_map/reduce_scatter | solution.py:144
  62.3 2.7 %copy-start.4 = (bf16[3456,256]{1,0:T(8,128)(2,1)S(1)}, bf16[3456,256]{1,0:T(8,128)(2,1)}, u32[]{:S(2)}) copy-start(bf16[3456,256]{1,0:T(8,128)(2,1)} %param.10) | copy-start | bytes 5308420
  74.0 65.5 %copy-start.2 = (f32[1024,128]{1,0:T(8,128)S(1)}, f32[1024,128]{1,0:T(8,128)}, u32[]{:S(2)}) copy-start(f32[1024,128]{1,0:T(8,128)} %get-tuple-element.222) | copy-start | bytes 1572868
  134.9 3.5 %copy-start.3 = (bf16[4,4,64,256]{3,2,1,0:T(8,128)(2,1)S(1)}, bf16[4,4,64,256]{3,2,1,0:T(8,128)(2,1)}, u32[]{:S(2)}) copy-start(bf16[4,4,64,256]{3,2,1,0:T(8,128)(2,1)} %get-tuple-element.165) | copy-start | bytes 1572868
Sparse Core Ops, SparseCore 0:
  55.7 79.1 reduce-scatter.2
  137.7 7.3 reduce-scatter.4
